TPU v7x, 32 devices: a whole 2x2x4 slice. The times are simulated.
32 devices in a mesh: grp: 2 (over x), node: 8 (over z, y), tm: 2 (over core).
Axes of the slice: x: 2, y: 2, z: 4, core: 2. Of those that a mesh axis runs over, the one named last changes fastest.
Arguments:
- scaled_kelvin: float32 [128, 8192], P(('grp', 'node', 'tm')), parts along dimension 0, may hold values from 0.5 to 1.5
- surface_emittance: float32 [16384], P('grp'), parts along dimension 0, may hold values from 0.2 to 1
- loss_factors: float32 [128, 8192], P(('grp', 'node', 'tm')), parts along dimension 0, may hold values from -6 to 6
- gebhart_tiles: bfloat16 [128, 32, 128, 128], P(('grp', 'node')), parts along dimension 0, may hold values from 1.4603138e-06 to 0.0014648438
- tile_target_index: int32 [128, 32], P(('grp', 'node')), parts along dimension 0, may hold values from 0 to 63
- tile_slots_occupied: int32 [128], P(('grp', 'node')), parts along dimension 0, may hold values from 16 to 32, as said below
Outputs:
- temp_sensitivity: float32 [128, 8192], P(('grp', 'node', 'tm')), parts along dimension 0
There are 2 independent parts, one for each index of `grp`. A program takes and returns all parts, laid end to end along the dimension named above; each array names one. Nothing has to cross between parts.
Inputs may be any that keep to these rules, and one draw needn't show every extreme that they name: A row's slots k below tile_slots_occupied are used, the others are ignored; some row of every variant uses all 32.
All inputs are finite; a program needn't handle non-finite values.
Results may differ from a plain program's by a relative error of at most 0.0036.
Values may be sent and summed in bfloat16 or wider, within the bound.
No kernel may reach another device: no remote copies, remote signals or barrier semaphores. Data moves between devices by JAX's collectives and lax.ppermute only.
A program may use at most 192 MiB of HBM per device.

v0:
```python
import jax
import jax.numpy as jnp
from jax import lax
from jax.sharding import PartitionSpec as P


def slot_window(gebhart_tiles, tile_target_index, tile_slots_occupied, slot_start, slot_width):
    in_use = (slot_start + jnp.arange(slot_width, dtype=jnp.int32))[None, :] < tile_slots_occupied[
        :, None
    ]
    return (gebhart_tiles, tile_target_index, in_use)


def over_slots(update, initial, slot_total):
    return update(initial, 0, slot_total)


def on_device(
    scaled_kelvin,
    surface_emittance,
    loss_factors,
    gebhart_tiles,
    tile_target_index,
    tile_slots_occupied,
):
    row_blocks, slot_total, block_side = (
        gebhart_tiles.shape[0],
        gebhart_tiles.shape[1],
        gebhart_tiles.shape[2],
    )
    surface_range = scaled_kelvin.shape[1]
    blocks_all = surface_range // block_side
    own_width = row_blocks * block_side
    own_start = lax.axis_index("node") * own_width
    radiant_output = (surface_emittance[None, :] * scaled_kelvin**4).astype(jnp.bfloat16)
    weights_here = lax.all_to_all(loss_factors, "node", split_axis=1, concat_axis=0, tiled=True)
    panel_rows = lax.all_gather(radiant_output, "node", axis=0, tiled=True)
    row_count = panel_rows.shape[0]
    panel_view = panel_rows.reshape(row_count, blocks_all, block_side)

    def update(running, slot_start, slot_width):
        tiles, columns, in_use = slot_window(
            gebhart_tiles, tile_target_index, tile_slots_occupied, slot_start, slot_width
        )
        picked = jnp.take(panel_view, columns.reshape(-1), axis=1)
        picked = picked.reshape(row_count, row_blocks, slot_width, block_side)
        picked = picked * in_use[None, :, :, None].astype(jnp.bfloat16)
        return jnp.einsum("nrkj,rkij->rni", picked, tiles, preferred_element_type=jnp.float32)

    flux = over_slots(
        update, jnp.zeros((row_blocks, row_count, block_side), jnp.float32), slot_total
    )
    flux = flux.transpose(1, 0, 2).reshape(row_count, own_width)
    own_emit = lax.dynamic_slice_in_dim(panel_rows, own_start, own_width, 1).astype(jnp.float32)
    weight_part = weights_here
    weight = weight_part * (flux - own_emit)
    sample_total = weight.shape[0]
    weight_rows = (
        weight.astype(jnp.bfloat16).reshape(sample_total, row_blocks, block_side).transpose(1, 0, 2)
    )
    weight_part = weight_rows

    def update(running, slot_start, slot_width):
        tiles, columns, in_use = slot_window(
            gebhart_tiles, tile_target_index, tile_slots_occupied, slot_start, slot_width
        )
        contrib = jnp.einsum(
            "rni,rkij->nrkj", weight_part, tiles, preferred_element_type=jnp.float32
        )
        targets = jnp.where(in_use, columns, blocks_all).reshape(-1)
        contrib = contrib.reshape(sample_total, row_blocks * slot_width, block_side)
        return running.at[:, targets, :].add(contrib, mode="drop")

    collected = over_slots(
        update, jnp.zeros((sample_total, blocks_all, block_side), jnp.float32), slot_total
    )
    summed = (
        lax.psum_scatter(
            collected.reshape(sample_total, surface_range).astype(jnp.bfloat16),
            "node",
            scatter_dimension=1,
            tiled=True,
        ).astype(jnp.float32)
        - weight
    )
    costate_vector = lax.all_to_all(summed, "node", split_axis=0, concat_axis=1, tiled=True)
    return 4.0 * surface_emittance[None, :] * scaled_kelvin**3 * costate_vector


def solution(mesh):
    placed = (
        P(("grp", "node", "tm"), None),
        P("grp"),
        P(("grp", "node", "tm"), None),
        P(("grp", "node"), None, None, None),
        P(("grp", "node"), None),
        P(("grp", "node")),
    )
    return jax.shard_map(
        on_device,
        mesh=mesh,
        in_specs=placed,
        out_specs=P(("grp", "node", "tm"), None),
        check_vma=False,
    )
```

profile of v0, /device:TPU:0, one launch (start us, length us, event | category | flops | bytes accessed | tf_op | source)
XLA Modules:
  0.0 169.4 jit_solution(2546197744501569730)
XLA Ops:
  6.5 7.3 %all-to-all-start = ((f32[4,8,1024]{2,0,1:T(4,128)}), f32[4,8,1024]{2,0,1:T(4,128)S(1)}, u32[]{:S(2)}, u32[]{:S(2)}) async-start(f32[4,8,1024]{2,0,1:T(4,128)} %bitcast.50), calls=%async_computation | async-start | bytes 262144 | tf_op jit(solution)/shard_map/all_to_all | solution.py:36
  13.8 0.0 reduce-scatter.2.cloned.1.call-start
  13.9 0.9 fusion.14
  14.8 31.9 %all-gather = bf16[8,4,8192]{2,1,0:T(4,128)(2,1)S(1)} all-gather(bf16[1,4,8192]{2,1,0:T(4,128)(2,1)S(1)} %fusion.14), channel_id=1, replica_groups=mesh['grp'=2,'node'=8,'tm'=2] {'node'}, dimensions={0}, use_global_device_ids=true | all-gather | bytes 589824 | tf_op jit(solution)/shard_map/all_gather | solution.py:37
  46.7 0.5 reshape.117
  47.3 0.3 copy.19
  47.6 0.8 reshape.118
  48.4 0.8 fusion.17
  49.2 1.0 gather_fusion
  50.2 0.0 copy-start.2
  50.2 0.0 copy-start.3
  50.2 5.2 %fusion.4 = f32[8,4,8,128]{3,2,1,0:T(8,128)S(1)} fusion(bf16[8,32,128,128]{3,2,1,0:T(8,128)(2,1)} %param.9, bf16[32,8,32,128]{3,0,2,1:T(8,128)(2,1)S(1)} %bitcast.46, pred[8,32]{1,0:T(8,128)(4,1)S(1)} %get-tuple-element.6, bf16[8,32]{1,0:T(8,128)(2,1)S(1)} %get-tuple-element.5), kind=kOutput, calls=%fused_computation.6 | convolution fusion | flops 270532608 | bytes 10617600 | tf_op jit(solution)/shard_map/nrkj,rkij->rni/dot_general | solution.py:48
  55.4 0.0 copy-done.2
  55.4 0.0 copy-done.3
  55.4 0.1 fusion.18
  55.5 0.1 reshape.139
  55.6 0.1 reshape.116
  55.7 0.0 all-to-all-done
  55.8 6.6 %fusion.15 = f32[8,32,32,128]{3,1,2,0:T(8,128)} fusion(bf16[8,32,128,128]{3,2,1,0:T(8,128)(2,1)} %param.9, bf16[8,32,128,1]{2,0,1,3:T(8,128)(2,1)S(1)} %bitcast.49), kind=kOutput, calls=%fused_computation.21 | convolution fusion | flops 268435456 | bytes 12648448 | tf_op jit(solution)/shard_map/rni,rkij->nrkj/dot_general | solution.py:67
  62.4 0.1 broadcast_in_dim.16
  62.5 0.0 copy-start.1
  62.5 0.0 copy-start
  62.5 22.6 %scatter_fusion = f32[32,64,128]{2,0,1:T(8,128)S(1)} fusion(f32[32,64,128]{2,0,1:T(8,128)S(1)} %broadcast_in_dim.16, s32[256]{0:T(256)S(1)} %bitcast.51, f32[256,32,128]{2,1,0:T(8,128)} %bitcast.45), kind=kCustom, calls=%fused_computation.1 | custom fusion | flops 1048576 | bytes 12583936 | tf_op jit(solution)/shard_map/scatter-add | solution.py:72
  85.1 0.8 copy_bitcast_fusion
  86.0 0.0 reduce-scatter.2.cloned.1.call-update
  86.0 63.3 %reduce-scatter.2.cloned.1.call-done = bf16[32,1024]{1,0:T(8,128)(2,1)} async-done(((bf16[32,8192]{1,0:T(8,128)(2,1)}), bf16[32,1024]{1,0:T(8,128)(2,1)}) %reduce-scatter.2.cloned.1.call-update) | async-done | bytes 65552 | tf_op jit(solution)/shard_map/reduce_scatter | solution.py:78
  149.3 0.9 convert_subtract_fusion
  150.2 0.7 all_to_all.32
  150.9 3.6 %all-to-all-start.1 = ((f32[8,4,1024]{2,1,0:T(4,128)}), f32[8,4,1024]{2,1,0:T(4,128)S(1)}, u32[]{:S(2)}, u32[]{:S(2)}) async-start(f32[8,4,1024]{2,1,0:T(4,128)} %all_to_all.32), calls=%async_computation.2 | async-start | bytes 262144 | tf_op jit(solution)/shard_map/all_to_all | solution.py:86
  154.5 0.0 copy-done.1
  154.5 7.3 %all-to-all-done.1 = f32[8,4,1024]{2,1,0:T(4,128)S(1)} async-done(((f32[8,4,1024]{2,1,0:T(4,128)}), f32[8,4,1024]{2,1,0:T(4,128)S(1)}, u32[]{:S(2)}, u32[]{:S(2)}) %all-to-all-start.1) | async-done | bytes 131104 | tf_op jit(solution)/shard_map/all_to_all | solution.py:86
  161.9 0.0 copy-done
  161.9 0.7 fusion.10
  (7 shorter events, 0.1 us)
Async XLA Ops:
  6.5 49.2 %all-to-all-start = ((f32[4,8,1024]{2,0,1:T(4,128)}), f32[4,8,1024]{2,0,1:T(4,128)S(1)}, u32[]{:S(2)}, u32[]{:S(2)}) async-start(f32[4,8,1024]{2,0,1:T(4,128)} %bitcast.50), calls=%async_computation | async-start | bytes 262144 | tf_op jit(solution)/shard_map/all_to_all | solution.py:36
  13.8 135.5 %reduce-scatter.2.cloned.1.call-start = ((), (), s32[]{:S(2)}) async-start(), calls=%async_computation.3 | async-start | bytes 589824 | tf_op jit(solution)/shard_map/reduce_scatter | solution.py:78
  50.2 5.2 %copy-start.2 = (s32[8,32]{1,0:T(8,128)S(1)}, s32[8,32]{1,0:T(8,128)}, u32[]{:S(2)}) copy-start(s32[8,32]{1,0:T(8,128)} %param.10) | copy-start | bytes 3076
  50.2 5.2 %copy-start.3 = (s32[8]{0:T(128)S(1)}, s32[8]{0:T(128)}, u32[]{:S(2)}) copy-start(s32[8]{0:T(128)} %param.11) | copy-start | bytes 100
  62.5 92.0 %copy-start.1 = (f32[8192]{0:T(1024)S(1)}, f32[8192]{0:T(1024)}, u32[]{:S(2)}) copy-start(f32[8192]{0:T(1024)} %param.7) | copy-start | bytes 98308
  62.5 99.3 %copy-start = (f32[4,8192]{1,0:T(4,128)S(1)}, f32[4,8192]{1,0:T(4,128)}, u32[]{:S(2)}) copy-start(f32[4,8192]{1,0:T(4,128)} %param.6) | copy-start | bytes 393220
  150.9 11.0 %all-to-all-start.1 = ((f32[8,4,1024]{2,1,0:T(4,128)}), f32[8,4,1024]{2,1,0:T(4,128)S(1)}, u32[]{:S(2)}, u32[]{:S(2)}) async-start(f32[8,4,1024]{2,1,0:T(4,128)} %all_to_all.32), calls=%async_computation.2 | async-start | bytes 262144 | tf_op jit(solution)/shard_map/all_to_all | solution.py:86
Sparse Core Ops, SparseCore 0:
  86.1 63.1 reduce-scatter.1
where the time goes:
time: 170 us; the launch traced here: 169 us
  waiting for transfers between devices  70.7 us (42%)
  blocking collectives  31.9 us (19%)
  other arithmetic  26.8 us (16%)
  between operations  13.5 us (8%)
  matrix products  11.7 us (7%)
  starting transfers between devices  10.9 us (6%)
  local copies, waits for them, and re-layouts  3.74 us (2%)
    reduce_scatter x1, waiting for transfers between devices, on_device(): lax.psum_scatter(collected.reshape(sample_total, surface_range).astype(jn...  63.3 us
    all_gather x1, blocking collectives, on_device(): panel_rows = lax.all_gather(radiant_output, 'node', axis=0, tiled=True)  31.9 us
    scatter-add x1, other arithmetic, update(): return running.at[:, targets, :].add(contrib, mode='drop')  22.6 us
    all_to_all x1, waiting for transfers between devices, on_device(): lax.all_to_all(summed, 'node', split_axis=0, concat_axis=1, tiled=True)  7.33 us
    all_to_all x1, starting transfers between devices, on_device(): lax.all_to_all(loss_factors, 'node', split_axis=1, concat_axis=0, tiled=T...  7.28 us
    dot_general x1, matrix products, update(): jnp.einsum('rni,rkij->nrkj', weight_part, tiles, preferred_element_type=j...  6.55 us
    dot_general x1, matrix products, update(): jnp.einsum('nrkj,rkij->rni', picked, tiles, preferred_element_type=jnp.fl...  5.19 us
    all_to_all x1, starting transfers between devices, on_device(): lax.all_to_all(summed, 'node', split_axis=0, concat_axis=1, tiled=True)  3.62 us
  transfers between devices with their start and end apart: 3, of which 2 were waited for; matrix products, arithmetic and copies ran while one was open for 6% of the time, Pallas kernels for 0%

commit v1 on v0

--- a/solution.py
+++ b/solution.py
@@ -2,6 +2,30 @@
 import jax.numpy as jnp
 from jax import lax
 from jax.sharding import PartitionSpec as P
+from jax.lax import axis_index, ppermute, psum
+
+
+def meet_sheets(array_here):
+    a_now = psum(1, "node")
+    outcome_arr = axis_index("node")
+    y2, q_next, r_now = (a_now, outcome_arr, array_here.shape[0])
+    all_blocks = tuple(((dev, (dev + 1) % y2) for dev in range(y2)))
+    parts_seen = tuple(((dev, (dev - 1) % y2) for dev in range(y2)))
+    fresh = jnp.zeros((*array_here.shape[:0], y2 * r_now, *array_here.shape[1:]), array_here.dtype)
+    fresh = lax.dynamic_update_slice_in_dim(fresh, array_here, q_next * r_now, axis=0)
+    response = piece_next = array_here
+    side_arr = y2 // 2
+    u = 1
+    while u < side_arr + 1:
+        response = ppermute(response, "node", all_blocks)
+        fresh = lax.dynamic_update_slice_in_dim(fresh, response, (q_next - u) % y2 * r_now, axis=0)
+        if u < y2 - side_arr:
+            piece_next = ppermute(piece_next, "node", parts_seen)
+            fresh = lax.dynamic_update_slice_in_dim(
+                fresh, piece_next, (q_next + u) % y2 * r_now, axis=0
+            )
+        u = u + 1
+    return fresh
 
 
 def slot_window(gebhart_tiles, tile_target_index, tile_slots_occupied, slot_start, slot_width):
@@ -34,7 +58,7 @@
     own_start = lax.axis_index("node") * own_width
     radiant_output = (surface_emittance[None, :] * scaled_kelvin**4).astype(jnp.bfloat16)
     weights_here = lax.all_to_all(loss_factors, "node", split_axis=1, concat_axis=0, tiled=True)
-    panel_rows = lax.all_gather(radiant_output, "node", axis=0, tiled=True)
+    panel_rows = meet_sheets(radiant_output)
     row_count = panel_rows.shape[0]
     panel_view = panel_rows.reshape(row_count, blocks_all, block_side)
 

time: 170 us -> 158 us (0.929)
  blocking collectives: 31.9 us -> 0 us
  starting transfers between devices: 10.9 us -> 22.6 us
  waiting for transfers between devices: 70.7 us -> 78.3 us
    all_gather x1 -> x0, blocking collectives: 31.9 us -> none  [on_device(): panel_rows = lax.all_gather(radiant_output, 'node', axis=0, tiled=True)]
    ppermute x0 -> x7, starting transfers between devices: none -> 15.6 us  [the longest x3 10.8 us: meet_sheets(): piece_next = ppermute(piece_next, 'node', parts_seen)]
    ppermute x0 -> x7, waiting for transfers between devices: none -> 11 us  [the longest x4 11 us: meet_sheets(): response = ppermute(response, 'node', all_blocks)]
    all_to_all x1, starting transfers between devices: 7.28 us -> 3.37 us  [on_device(): lax.all_to_all(loss_factors, 'node', split_axis=1, concat_axis=0, tiled=T...]
    reduce_scatter x1, waiting for transfers between devices: 63.3 us -> 59.9 us  [on_device(): lax.psum_scatter(collected.reshape(sample_total, surface_range).astype(jn...]
  transfers between devices with their start and end apart: 3 -> 10, of which waited for: 2 -> 5; matrix products, arithmetic and copies ran while one was open for 6% -> 2% of each run, Pallas kernels for 0% -> 0%
where the time goes in v1:
time: 158 us; the launch traced here: 157 us
  waiting for transfers between devices  78.3 us (50%)
  other arithmetic  27.6 us (17%)
  starting transfers between devices  22.6 us (14%)
  between operations  13.7 us (9%)
  matrix products  11.7 us (7%)
  local copies, waits for them, and re-layouts  3.19 us (2%)
    reduce_scatter x1, waiting for transfers between devices, on_device(): lax.psum_scatter(collected.reshape(sample_total, surface_range).astype(jn...  59.9 us
    scatter-add x1, other arithmetic, update(): return running.at[:, targets, :].add(contrib, mode='drop')  22.6 us
    ppermute x4, waiting for transfers between devices, meet_sheets(): response = ppermute(response, 'node', all_blocks)  11 us
    ppermute x3, starting transfers between devices, meet_sheets(): piece_next = ppermute(piece_next, 'node', parts_seen)  10.8 us
    all_to_all x1, waiting for transfers between devices, on_device(): lax.all_to_all(summed, 'node', split_axis=0, concat_axis=1, tiled=True)  7.33 us
    dot_general x1, matrix products, update(): jnp.einsum('rni,rkij->nrkj', weight_part, tiles, preferred_element_type=j...  6.56 us
    dot_general x1, matrix products, update(): jnp.einsum('nrkj,rkij->rni', picked, tiles, preferred_element_type=jnp.fl...  5.19 us
    ppermute x4, starting transfers between devices, meet_sheets(): response = ppermute(response, 'node', all_blocks)  4.83 us
  transfers between devices with their start and end apart: 10, of which 5 were waited for; matrix products, arithmetic and copies ran while one was open for 2% of the time, Pallas kernels for 0%

profile of v1, /device:TPU:0, one launch (start us, length us, event | category | flops | bytes accessed | tf_op | source)
XLA Modules:
  0.0 157.1 jit_solution(10213907895184045333)
XLA Ops:
  6.6 1.0 constant_dynamic-update-slice_fusion.7
  7.6 3.0 %collective-permute-start = (bf16[4,8192]{1,0:T(4,128)(2,1)S(1)}, bf16[4,8192]{1,0:T(4,128)(2,1)S(1)}, u32[]{:S(2)}, u32[]{:S(2)}) collective-permute-start(bf16[4,8192]{1,0:T(4,128)(2,1)S(1)} %get-tuple-element.6), channel_id=1, source_target_pairs={{0,2},{2,4},{4,6},{6,8},{8,10},{10,12},{12,14},{14,0},{1,3},{3,5},... | collective-permute-start | bytes 196616 | tf_op jit(solution)/shard_map/ppermute | solution.py:20
  10.6 3.1 %collective-permute-start.1 = (bf16[4,8192]{1,0:T(4,128)(2,1)S(1)}, bf16[4,8192]{1,0:T(4,128)(2,1)S(1)}, u32[]{:S(2)}, u32[]{:S(2)}) collective-permute-start(bf16[4,8192]{1,0:T(4,128)(2,1)S(1)} %get-tuple-element.6), channel_id=1, source_target_pairs={{0,14},{2,0},{4,2},{6,4},{8,6},{10,8},{12,10},{14,12},{1,15},{3,1}... | collective-permute-start | bytes 196616 | tf_op jit(solution)/shard_map/ppermute | solution.py:23
  13.7 3.4 %all-to-all-start = ((f32[4,8,1024]{2,0,1:T(4,128)}), f32[4,8,1024]{2,0,1:T(4,128)S(1)}, u32[]{:S(2)}, u32[]{:S(2)}) async-start(f32[4,8,1024]{2,0,1:T(4,128)} %bitcast.53), calls=%async_computation | async-start | bytes 262144 | tf_op jit(solution)/shard_map/all_to_all | solution.py:60
  17.1 0.0 reduce-scatter.2.cloned.1.call-start
  17.2 0.8 reshape.118
  18.0 0.8 fusion.17
  18.8 0.8 fusion.16
  19.5 0.1 reshape.116
  19.6 0.0 collective-permute-done
  19.6 1.8 %collective-permute-start.2 = (bf16[4,8192]{1,0:T(4,128)(2,1)S(1)}, bf16[4,8192]{1,0:T(4,128)(2,1)S(1)}, u32[]{:S(2)}, u32[]{:S(2)}) collective-permute-start(bf16[4,8192]{1,0:T(4,128)(2,1)S(1)} %collective-permute-done), channel_id=1, source_target_pairs={{0,2},{2,4},{4,6},{6,8},{8,10},{10,12},{12,14},{14,0},{1,3},{3,5},... | collective-permute-start | bytes 196616 | tf_op jit(solution)/shard_map/ppermute | solution.py:20
  21.4 0.0 collective-permute-done.1
  21.4 3.0 %collective-permute-start.3 = (bf16[4,8192]{1,0:T(4,128)(2,1)S(1)}, bf16[4,8192]{1,0:T(4,128)(2,1)S(1)}, u32[]{:S(2)}, u32[]{:S(2)}) collective-permute-start(bf16[4,8192]{1,0:T(4,128)(2,1)S(1)} %collective-permute-done.1), channel_id=1, source_target_pairs={{0,14},{2,0},{4,2},{6,4},{8,6},{10,8},{12,10},{14,12},{1,15},{3,1}... | collective-permute-start | bytes 196616 | tf_op jit(solution)/shard_map/ppermute | solution.py:23
  24.5 0.1 constant_dynamic-update-slice_fusion.5
  24.5 2.1 %collective-permute-done.2 = bf16[4,8192]{1,0:T(4,128)(2,1)S(1)} collective-permute-done((bf16[4,8192]{1,0:T(4,128)(2,1)S(1)}, bf16[4,8192]{1,0:T(4,128)(2,1)S(1)}, u32[]{:S(2)}, u32[]{:S(2)}) %collective-permute-start.2) | collective-permute-done | bytes 65568 | tf_op jit(solution)/shard_map/ppermute | solution.py:20
  26.7 0.0 collective-permute-start.4
  26.7 0.0 collective-permute-done.3
  26.7 4.7 %collective-permute-start.5 = (bf16[4,8192]{1,0:T(4,128)(2,1)S(1)}, bf16[4,8192]{1,0:T(4,128)(2,1)S(1)}, u32[]{:S(2)}, u32[]{:S(2)}) collective-permute-start(bf16[4,8192]{1,0:T(4,128)(2,1)S(1)} %collective-permute-done.3), channel_id=1, source_target_pairs={{0,14},{2,0},{4,2},{6,4},{8,6},{10,8},{12,10},{14,12},{1,15},{3,1}... | collective-permute-start | bytes 196616 | tf_op jit(solution)/shard_map/ppermute | solution.py:23
  31.4 0.1 constant_dynamic-update-slice_fusion.3
  31.5 2.1 %collective-permute-done.4 = bf16[4,8192]{1,0:T(4,128)(2,1)S(1)} collective-permute-done((bf16[4,8192]{1,0:T(4,128)(2,1)S(1)}, bf16[4,8192]{1,0:T(4,128)(2,1)S(1)}, u32[]{:S(2)}, u32[]{:S(2)}) %collective-permute-start.4) | collective-permute-done | bytes 65568 | tf_op jit(solution)/shard_map/ppermute | solution.py:20
  33.6 0.0 collective-permute-start.6
  33.7 0.0 collective-permute-done.5
  33.7 0.1 constant_dynamic-update-slice_fusion.1
  33.7 0.0 all-to-all-done
  33.8 6.8 %collective-permute-done.6 = bf16[4,8192]{1,0:T(4,128)(2,1)S(1)} collective-permute-done((bf16[4,8192]{1,0:T(4,128)(2,1)S(1)}, bf16[4,8192]{1,0:T(4,128)(2,1)S(1)}, u32[]{:S(2)}, u32[]{:S(2)}) %collective-permute-start.6) | collective-permute-done | bytes 65568 | tf_op jit(solution)/shard_map/ppermute | solution.py:20
  40.6 0.1 copy_bitcast_fusion.1
  40.7 1.0 gather_fusion
  41.7 5.2 %fusion.4 = f32[8,4,8,128]{3,2,1,0:T(8,128)S(1)} fusion(bf16[8,32,128,128]{3,2,1,0:T(8,128)(2,1)} %param.9, bf16[32,8,32,128]{3,0,2,1:T(8,128)(2,1)S(1)} %bitcast.49, pred[8,32]{1,0:T(8,128)(4,1)S(1)} %get-tuple-element.10, bf16[8,32]{1,0:T(8,128)(2,1)S(1)} %get-tuple-element.9), kind=kOutput, calls=%fused_computation.6 | convolution fusion | flops 270532608 | bytes 10617600 | tf_op jit(solution)/shard_map/nrkj,rkij->rni/dot_general | solution.py:72
  47.0 6.6 %fusion.14 = f32[8,32,32,128]{3,1,2,0:T(8,128)} fusion(bf16[8,32,128,128]{3,2,1,0:T(8,128)(2,1)} %param.9, bf16[8,32,128,1]{2,0,1,3:T(8,128)(2,1)S(1)} %bitcast.52), kind=kOutput, calls=%fused_computation.21 | convolution fusion | flops 268435456 | bytes 12648448 | tf_op jit(solution)/shard_map/rni,rkij->nrkj/dot_general | solution.py:91
  53.6 0.1 broadcast_in_dim.28
  53.7 0.0 copy-start.1
  53.7 0.0 copy-start
  53.7 22.6 %scatter_fusion = f32[32,64,128]{2,0,1:T(8,128)S(1)} fusion(f32[32,64,128]{2,0,1:T(8,128)S(1)} %broadcast_in_dim.28, s32[256]{0:T(256)S(1)} %bitcast.54, f32[256,32,128]{2,1,0:T(8,128)} %bitcast.48), kind=kCustom, calls=%fused_computation.1 | custom fusion | flops 1048576 | bytes 12583936 | tf_op jit(solution)/shard_map/scatter-add | solution.py:96
  76.3 0.8 copy_bitcast_fusion
  77.1 0.0 reduce-scatter.2.cloned.1.call-update
  77.2 59.9 %reduce-scatter.2.cloned.1.call-done = bf16[32,1024]{1,0:T(8,128)(2,1)} async-done(((bf16[32,8192]{1,0:T(8,128)(2,1)}), bf16[32,1024]{1,0:T(8,128)(2,1)}) %reduce-scatter.2.cloned.1.call-update) | async-done | bytes 65552 | tf_op jit(solution)/shard_map/reduce_scatter | solution.py:102
  137.1 0.9 convert_subtract_fusion
  137.9 0.7 all_to_all.32
  138.6 3.6 %all-to-all-start.1 = ((f32[8,4,1024]{2,1,0:T(4,128)}), f32[8,4,1024]{2,1,0:T(4,128)S(1)}, u32[]{:S(2)}, u32[]{:S(2)}) async-start(f32[8,4,1024]{2,1,0:T(4,128)} %all_to_all.32), calls=%async_computation.2 | async-start | bytes 262144 | tf_op jit(solution)/shard_map/all_to_all | solution.py:110
  142.2 0.0 copy-done.1
  142.2 7.3 %all-to-all-done.1 = f32[8,4,1024]{2,1,0:T(4,128)S(1)} async-done(((f32[8,4,1024]{2,1,0:T(4,128)}), f32[8,4,1024]{2,1,0:T(4,128)S(1)}, u32[]{:S(2)}, u32[]{:S(2)}) %all-to-all-start.1) | async-done | bytes 131104 | tf_op jit(solution)/shard_map/all_to_all | solution.py:110
  149.6 0.0 copy-done
  149.6 0.7 fusion.10
  (11 shorter events, 0.3 us)
Async XLA Ops:
  7.6 12.1 %collective-permute-start = (bf16[4,8192]{1,0:T(4,128)(2,1)S(1)}, bf16[4,8192]{1,0:T(4,128)(2,1)S(1)}, u32[]{:S(2)}, u32[]{:S(2)}) collective-permute-start(bf16[4,8192]{1,0:T(4,128)(2,1)S(1)} %get-tuple-element.6), channel_id=1, source_target_pairs={{0,2},{2,4},{4,6},{6,8},{8,10},{10,12},{12,14},{14,0},{1,3},{3,5},... | collective-permute-start | bytes 196616 | tf_op jit(solution)/shard_map/ppermute | solution.py:20
  10.6 10.9 %collective-permute-start.1 = (bf16[4,8192]{1,0:T(4,128)(2,1)S(1)}, bf16[4,8192]{1,0:T(4,128)(2,1)S(1)}, u32[]{:S(2)}, u32[]{:S(2)}) collective-permute-start(bf16[4,8192]{1,0:T(4,128)(2,1)S(1)} %get-tuple-element.6), channel_id=1, source_target_pairs={{0,14},{2,0},{4,2},{6,4},{8,6},{10,8},{12,10},{14,12},{1,15},{3,1}... | collective-permute-start | bytes 196616 | tf_op jit(solution)/shard_map/ppermute | solution.py:23
  13.7 20.1 %all-to-all-start = ((f32[4,8,1024]{2,0,1:T(4,128)}), f32[4,8,1024]{2,0,1:T(4,128)S(1)}, u32[]{:S(2)}, u32[]{:S(2)}) async-start(f32[4,8,1024]{2,0,1:T(4,128)} %bitcast.53), calls=%async_computation | async-start | bytes 262144 | tf_op jit(solution)/shard_map/all_to_all | solution.py:60
  17.1 120.0 %reduce-scatter.2.cloned.1.call-start = ((), (), s32[]{:S(2)}) async-start(), calls=%async_computation.3 | async-start | bytes 589824 | tf_op jit(solution)/shard_map/reduce_scatter | solution.py:102
  19.6 7.0 %collective-permute-start.2 = (bf16[4,8192]{1,0:T(4,128)(2,1)S(1)}, bf16[4,8192]{1,0:T(4,128)(2,1)S(1)}, u32[]{:S(2)}, u32[]{:S(2)}) collective-permute-start(bf16[4,8192]{1,0:T(4,128)(2,1)S(1)} %collective-permute-done), channel_id=1, source_target_pairs={{0,2},{2,4},{4,6},{6,8},{8,10},{10,12},{12,14},{14,0},{1,3},{3,5},... | collective-permute-start | bytes 196616 | tf_op jit(solution)/shard_map/ppermute | solution.py:20
  21.4 5.2 %collective-permute-start.3 = (bf16[4,8192]{1,0:T(4,128)(2,1)S(1)}, bf16[4,8192]{1,0:T(4,128)(2,1)S(1)}, u32[]{:S(2)}, u32[]{:S(2)}) collective-permute-start(bf16[4,8192]{1,0:T(4,128)(2,1)S(1)} %collective-permute-done.1), channel_id=1, source_target_pairs={{0,14},{2,0},{4,2},{6,4},{8,6},{10,8},{12,10},{14,12},{1,15},{3,1}... | collective-permute-start | bytes 196616 | tf_op jit(solution)/shard_map/ppermute | solution.py:23
  26.7 7.0 %collective-permute-start.4 = (bf16[4,8192]{1,0:T(4,128)(2,1)S(1)}, bf16[4,8192]{1,0:T(4,128)(2,1)S(1)}, u32[]{:S(2)}, u32[]{:S(2)}) collective-permute-start(bf16[4,8192]{1,0:T(4,128)(2,1)S(1)} %collective-permute-done.2), channel_id=1, source_target_pairs={{0,2},{2,4},{4,6},{6,8},{8,10},{10,12},{12,14},{14,0},{1,3},{3,5},... | collective-permute-start | bytes 196616 | tf_op jit(solution)/shard_map/ppermute | solution.py:20
  26.7 7.0 %collective-permute-start.5 = (bf16[4,8192]{1,0:T(4,128)(2,1)S(1)}, bf16[4,8192]{1,0:T(4,128)(2,1)S(1)}, u32[]{:S(2)}, u32[]{:S(2)}) collective-permute-start(bf16[4,8192]{1,0:T(4,128)(2,1)S(1)} %collective-permute-done.3), channel_id=1, source_target_pairs={{0,14},{2,0},{4,2},{6,4},{8,6},{10,8},{12,10},{14,12},{1,15},{3,1}... | collective-permute-start | bytes 196616 | tf_op jit(solution)/shard_map/ppermute | solution.py:23
  33.6 7.0 %collective-permute-start.6 = (bf16[4,8192]{1,0:T(4,128)(2,1)S(1)}, bf16[4,8192]{1,0:T(4,128)(2,1)S(1)}, u32[]{:S(2)}, u32[]{:S(2)}) collective-permute-start(bf16[4,8192]{1,0:T(4,128)(2,1)S(1)} %collective-permute-done.4), channel_id=1, source_target_pairs={{0,2},{2,4},{4,6},{6,8},{8,10},{10,12},{12,14},{14,0},{1,3},{3,5},... | collective-permute-start | bytes 196616 | tf_op jit(solution)/shard_map/ppermute | solution.py:20
  53.7 88.5 %copy-start.1 = (f32[8192]{0:T(1024)S(1)}, f32[8192]{0:T(1024)}, u32[]{:S(2)}) copy-start(f32[8192]{0:T(1024)} %param.7) | copy-start | bytes 98308
  53.7 95.9 %copy-start = (f32[4,8192]{1,0:T(4,128)S(1)}, f32[4,8192]{1,0:T(4,128)}, u32[]{:S(2)}) copy-start(f32[4,8192]{1,0:T(4,128)} %param.6) | copy-start | bytes 393220
  138.6 10.9 %all-to-all-start.1 = ((f32[8,4,1024]{2,1,0:T(4,128)}), f32[8,4,1024]{2,1,0:T(4,128)S(1)}, u32[]{:S(2)}, u32[]{:S(2)}) async-start(f32[8,4,1024]{2,1,0:T(4,128)} %all_to_all.32), calls=%async_computation.2 | async-start | bytes 262144 | tf_op jit(solution)/shard_map/all_to_all | solution.py:110
Sparse Core Ops, SparseCore 0:
  77.3 59.7 reduce-scatter.1
